TPU v7x, 32 devices: a whole 2x2x4 slice. The times are simulated.
32 devices in a mesh: groups: 2 (over y), expert: 4 (over z), token: 4 (over x, core).
Axes of the slice: x: 2, y: 2, z: 4, core: 2. Of those that a mesh axis runs over, the one named last changes fastest.
Arguments:
- tokens: bfloat16 [512, 2048], P(('groups', 'expert'), 'token'), parts along dimension 0, may hold values from -6 to 6
- expert_ids: int32 [512, 8], P(('groups', 'expert')), parts along dimension 0, may hold values from 0 to 15, all different within a row; in each aligned block of 64 rows (0 to 63, 64 to 127, ...) at most 64 rows name the same one
- route_weights: float32 [512, 8], P(('groups', 'expert')), parts along dimension 0, may hold values from 0.1 to 0.4
- w_gate_up: bfloat16 [16, 2048, 1536], P('expert', 'token'), may hold values from -0.125 to 0.125
- w_down: bfloat16 [16, 768, 2048], P('expert', None, 'token'), may hold values from -0.21875 to 0.21875
Outputs:
- combined: bfloat16 [512, 2048], P(('groups', 'expert'), 'token'), parts along dimension 0
There are 2 independent parts, one for each index of `groups`. A program takes and returns all parts, laid end to end along the dimension named above; an argument that names none is the same for every part. Nothing has to cross between parts.
Inputs may be any that keep to these rules, and one draw needn't show every extreme that they name: `expert_ids`: each row names 8 different experts. In each aligned block of 64 rows no expert is named by more than 64 rows, a bound that some block reaches.
All inputs are finite; a program needn't handle non-finite values.
Results may differ from a plain program's by a relative error of at most 0.02.
Values may be sent and summed in bfloat16 or wider, within the bound.
A program may use at most 64 MiB of HBM per device.

v0:
```python
import jax
import jax.numpy as jnp
from jax import lax
from jax.sharding import PartitionSpec as P


def rank_slots(flat_ids, experts):
    onehot = (flat_ids[:, None] == jnp.arange(experts, dtype=jnp.int32)[None, :]).astype(jnp.int32)
    rank_of = jnp.sum((jnp.cumsum(onehot, axis=0) - 1) * onehot, axis=1)
    return (onehot, rank_of)


def gate_up_terms(inputs, w_gate_up):
    return jnp.einsum("erd,edf->ref", inputs, w_gate_up, preferred_element_type=jnp.float32)


def expert_block(inputs, gate_up_w, down_w):
    hidden_units = gate_up_w.shape[2] // 2
    summed = lax.psum_scatter(
        gate_up_terms(inputs, gate_up_w).astype(jnp.bfloat16),
        "token",
        scatter_dimension=0,
        tiled=True,
    ).astype(jnp.float32)
    hidden = (jax.nn.silu(summed[..., :hidden_units]) * summed[..., hidden_units:]).astype(
        jnp.bfloat16
    )
    produced = jnp.einsum(
        "reh,ehd->erd",
        lax.all_gather(hidden, "token", axis=0, tiled=True),
        down_w,
        preferred_element_type=jnp.float32,
    )
    return produced.astype(jnp.bfloat16)


def per_device(tokens, expert_ids, route_weights, w_gate_up, w_down):
    tok_dev, feature_cols = tokens.shape
    top_k = expert_ids.shape[1]
    local_experts = w_gate_up.shape[0]
    n_expert = lax.axis_size("expert")
    experts = local_experts * n_expert
    capacity = max(2, min(tok_dev, tok_dev * top_k * 5 // (2 * experts)))
    slot_count = n_expert * capacity
    flat_ids = expert_ids.reshape(-1)
    onehot, rank_of = rank_slots(flat_ids, experts)
    position = (
        flat_ids % local_experts * slot_count + flat_ids // local_experts * capacity + rank_of
    )
    token_of = jnp.arange(flat_ids.shape[0], dtype=jnp.int32) // top_k
    slot_table = (
        jnp.full((local_experts * slot_count,), tok_dev, jnp.int32).at[position].set(token_of)
    )
    padded = jnp.concatenate([tokens, jnp.zeros((1, feature_cols), tokens.dtype)], axis=0)
    outgoing = jnp.take(padded, slot_table, axis=0).reshape(
        local_experts, n_expert, capacity, feature_cols
    )
    arrived = lax.all_to_all(outgoing, "expert", split_axis=1, concat_axis=1, tiled=True)
    inputs = arrived.reshape(local_experts, slot_count, feature_cols)
    expert_out = expert_block(inputs, w_gate_up, w_down)
    returned = lax.all_to_all(
        expert_out.reshape(local_experts, n_expert, capacity, feature_cols),
        "expert",
        split_axis=1,
        concat_axis=1,
        tiled=True,
    )
    picked = jnp.take(
        returned.reshape(local_experts * slot_count, feature_cols), position, axis=0
    ).reshape(tok_dev, top_k, feature_cols)
    combined = jnp.sum(route_weights[:, :, None] * picked.astype(jnp.float32), axis=1)
    return combined.astype(jnp.bfloat16)


def solution(mesh):
    return jax.shard_map(
        per_device,
        mesh=mesh,
        in_specs=(
            P(("groups", "expert"), "token"),
            P(("groups", "expert"), None),
            P(("groups", "expert"), None),
            P("expert", "token", None),
            P("expert", None, "token"),
        ),
        out_specs=P(("groups", "expert"), "token"),
        check_vma=False,
    )
```

profile of v0, /device:TPU:0, one launch (start us, length us, event | category | flops | bytes accessed | tf_op | source)
XLA Modules:
  0.0 166.3 jit_solution(5265012218865901291)
XLA Ops:
  6.5 0.9 copy.31
  7.5 0.1 eq.28
  7.6 0.1 reshape.180
  7.6 0.1 reshape.182
  7.8 1.2 reduce-window.6
  8.9 0.2 slice_reduce_fusion
  9.2 0.1 fusion.7
  9.3 2.4 %scatter_custom_fusion = s32[1024]{0:T(1024)S(1)} fusion(s32[512]{0:T(512)S(1)} %bitcast.36, s32[512]{0:T(512)S(1)} %add_select_fusion.2, s32[]{:T(128)} %constant.82.clone.1), kind=kCustom, calls=%fused_computation.54 | custom fusion | bytes 4100 | tf_op jit(solution)/shard_map/scatter | solution.py:52
  11.8 0.1 broadcast_in_dim.33
  11.9 0.8 concatenate.3
  12.7 5.1 %gather_fusion = bf16[1024,512]{1,0:T(8,128)(2,1)} fusion(bf16[65,512]{1,0:T(8,128)(2,1)S(1)} %concatenate.3, s32[1024]{0:T(1024)S(1)} %fusion.13), kind=kCustom, calls=%fused_computation | custom fusion | bytes 2101248 | tf_op jit(solution)/shard_map/jit(_take)/gather | solution.py:55
  17.8 1.4 copy_select_fusion
  19.2 31.9 %all_to_all.10 = bf16[4,4,64,512]{3,2,0,1:T(8,128)(2,1)S(1)} all-to-all(bf16[4,4,64,512]{3,2,0,1:T(8,128)(2,1)S(1)} %copy_select_fusion), channel_id=1, replica_groups=mesh['groups'=2,'expert'=4,'token'=4] {'expert'}, dimensions={1} | all-to-all | bytes 2097152 | tf_op jit(solution)/shard_map/all_to_all | solution.py:58
  51.1 0.1 copy.41
  51.2 6.3 %fusion = bf16[256,4,1536]{2,0,1:T(8,128)(2,1)} fusion(bf16[4,256,512]{2,1,0:T(8,128)(2,1)S(1)} %bitcast.33, bf16[4,512,1536]{2,1,0:T(8,128)(2,1)} %param.8), kind=kOutput, calls=%fused_computation.4 | convolution fusion | flops 1612185600 | bytes 10485760 | tf_op jit(solution)/shard_map/erd,edf->ref/dot_general | solution.py:14
  57.4 0.0 reduce-scatter.2.cloned.1.call-update
  57.5 0.0 all-gather.2.cloned.1.call-start
  57.5 37.0 %reduce-scatter.2.cloned.1.call-done = bf16[64,4,1536]{2,0,1:T(8,128)(2,1)} async-done(((bf16[256,4,1536]{2,0,1:T(8,128)(2,1)}), bf16[64,4,1536]{2,0,1:T(8,128)(2,1)}) %reduce-scatter.2.cloned.1.call-update) | async-done | bytes 786448 | tf_op jit(solution)/shard_map/reduce_scatter | solution.py:19
  94.5 1.3 convert_element_type.29
  95.8 1.0 fusion.1
  96.8 0.0 all-gather.2.cloned.1.call-update
  96.8 19.8 %all-gather.2.cloned.1.call-done = bf16[256,4,768]{2,0,1:T(8,128)(2,1)} async-done(((bf16[64,4,768]{2,0,1:T(8,128)(2,1)}), bf16[256,4,768]{2,0,1:T(8,128)(2,1)}) %all-gather.2.cloned.1.call-update) | async-done | bytes 1572880 | tf_op jit(solution)/shard_map/all_gather | solution.py:30
  116.6 2.4 %convolution_convert_fusion.1 = bf16[4,256,512]{2,1,0:T(8,128)(2,1)S(1)} fusion(bf16[256,4,768]{2,0,1:T(8,128)(2,1)} %all-gather.2.cloned.1.call-done, bf16[4,768,512]{2,1,0:T(8,128)(2,1)S(1)} %copy-done), kind=kOutput, calls=%fused_computation.5 | convolution fusion | flops 805830656 | bytes 5767168 | tf_op jit(solution)/shard_map/reh,ehd->erd/dot_general | solution.py:28
  119.0 1.1 copy.42
  120.1 4.6 %all-to-all-start.1 = ((bf16[4,4,64,512]{3,2,0,1:T(8,128)(2,1)}), bf16[4,4,64,512]{3,2,0,1:T(8,128)(2,1)}, u32[]{:S(2)}, u32[]{:S(2)}) async-start(bf16[4,4,64,512]{3,2,0,1:T(8,128)(2,1)} %copy.42), calls=%async_computation.2 | async-start | bytes 2097152 | tf_op jit(solution)/shard_map/all_to_all | solution.py:61
  124.7 0.1 reduce_sum.23
  124.8 0.1 copy.30
  124.9 0.1 compare_and_fusion
  125.0 26.0 %all-to-all-done.1 = bf16[4,4,64,512]{3,2,0,1:T(8,128)(2,1)} async-done(((bf16[4,4,64,512]{3,2,0,1:T(8,128)(2,1)}), bf16[4,4,64,512]{3,2,0,1:T(8,128)(2,1)}, u32[]{:S(2)}, u32[]{:S(2)}) %all-to-all-start.1) | async-done | bytes 1048608 | tf_op jit(solution)/shard_map/all_to_all | solution.py:61
  151.0 2.4 %copy.43 = bf16[4,4,64,512]{3,2,1,0:T(8,128)(2,1)} copy(bf16[4,4,64,512]{3,2,0,1:T(8,128)(2,1)} %all-to-all-done.1) | data formatting | bytes 2097152 | tf_op jit(solution)/shard_map/all_to_all | solution.py:61
  153.3 4.0 %gather_fusion.1 = bf16[512,512]{1,0:T(8,128)(2,1)} fusion(bf16[1024,512]{1,0:T(8,128)(2,1)} %bitcast.31, s32[1024]{0:T(1024)S(1)} %pad_clamp_fusion), kind=kCustom, calls=%fused_computation.1 | custom fusion | bytes 1050624 | tf_op jit(solution)/shard_map/jit(_take)/gather | solution.py:68
  157.3 2.1 %multiply_reduce_fusion = bf16[64,512]{1,0:T(8,128)(2,1)} fusion(bf16[512,512]{1,0:T(8,128)(2,1)} %gather_fusion.1, f32[64,8]{1,0:T(8,128)S(1)} %copy.30, pred[64,8]{1,0:T(8,128)(4,1)S(1)} %compare_and_fusion), kind=kLoop, calls=%fused_computation.7 | loop fusion | flops 1015808 | bytes 592384 | tf_op jit(solution)/shard_map/reduce_sum | solution.py:71
  (14 shorter events, 0.1 us)
Async XLA Ops:
  6.5 110.1 %copy-start = (bf16[4,768,512]{2,1,0:T(8,128)(2,1)S(1)}, bf16[4,768,512]{2,1,0:T(8,128)(2,1)}, u32[]{:S(2)}) copy-start(bf16[4,768,512]{2,1,0:T(8,128)(2,1)} %param.9) | copy-start | bytes 9437188
  6.5 88.0 %reduce-scatter.2.cloned.1.call-start = ((), (), s32[]{:S(2)}) async-start(), calls=%async_computation.3 | async-start | bytes 3932160 | tf_op jit(solution)/shard_map/reduce_scatter | solution.py:19
  57.5 59.1 %all-gather.2.cloned.1.call-start = ((), (), s32[]{:S(2)}) async-start(), calls=%async_computation.4 | async-start | bytes 1966080 | tf_op jit(solution)/shard_map/all_gather | solution.py:30
  119.0 5.8 %copy-start.1 = (f32[64,8]{0,1:T(8,128)S(1)}, f32[64,8]{0,1:T(8,128)}, u32[]{:S(2)}) copy-start(f32[64,8]{0,1:T(8,128)} %param.7) | copy-start | bytes 6148
  120.1 30.8 %all-to-all-start.1 = ((bf16[4,4,64,512]{3,2,0,1:T(8,128)(2,1)}), bf16[4,4,64,512]{3,2,0,1:T(8,128)(2,1)}, u32[]{:S(2)}, u32[]{:S(2)}) async-start(bf16[4,4,64,512]{3,2,0,1:T(8,128)(2,1)} %copy.42), calls=%async_computation.2 | async-start | bytes 2097152 | tf_op jit(solution)/shard_map/all_to_all | solution.py:61
Sparse Core Ops, SparseCore 0:
  57.6 36.8 reduce-scatter.1
  96.9 19.6 all-gather.1
where the time goes:
time: 167 us; the launch traced here: 166 us
  waiting for transfers between devices  82.8 us (50%)
  blocking collectives  31.9 us (19%)
  local copies, waits for them, and re-layouts  17.6 us (11%)
  between operations  13.5 us (8%)
  matrix products  8.66 us (5%)
  other arithmetic  7.2 us (4%)
  starting transfers between devices  4.64 us (3%)
    reduce_scatter x1, waiting for transfers between devices, expert_block(): lax.psum_scatter(gate_up_terms(inputs, gate_up_w).astype(jnp.bfloat16), '...  37 us
    all_to_all x1, blocking collectives, per_device(): lax.all_to_all(outgoing, 'expert', split_axis=1, concat_axis=1, tiled=True)  31.9 us
    all_to_all x1, waiting for transfers between devices, per_device(): lax.all_to_all(expert_out.reshape(local_experts, n_expert, capacity, feat...  26 us
    all_gather x1, waiting for transfers between devices, expert_block(): lax.all_gather(hidden, 'token', axis=0, tiled=True)  19.8 us
    dot_general x1, matrix products, gate_up_terms(): jnp.einsum('erd,edf->ref', inputs, w_gate_up, preferred_element_type=jnp....  6.28 us
    gather x1, local copies, waits for them, and re-layouts, per_device(): jnp.take(padded, slot_table, axis=0)  5.06 us
    all_to_all x1, starting transfers between devices, per_device(): lax.all_to_all(expert_out.reshape(local_experts, n_expert, capacity, feat...  4.6 us
    gather x1, local copies, waits for them, and re-layouts, per_device(): jnp.take(returned.reshape(local_experts * slot_count, feature_cols), posi...  4.01 us
  transfers between devices with their start and end apart: 3, of which 3 were waited for; matrix products, arithmetic and copies ran while one was open for 0% of the time, Pallas kernels for 0%

commit v1 on v0

--- a/solution.py
+++ b/solution.py
@@ -2,6 +2,28 @@
 import jax.numpy as jnp
 from jax import lax
 from jax.sharding import PartitionSpec as P
+
+
+def laid_out(tiles, dim):
+    tiles = jnp.moveaxis(tiles, 0, dim)
+    shape = tiles.shape
+    return tiles.reshape(*shape[:dim], shape[dim] * shape[dim + 1], *shape[dim + 2 :])
+
+
+def doubled(x, axis):
+    peers = lax.axis_size(axis)
+    parts = x[None]
+    for level in range(peers.bit_length() - 1):
+        distance = 1 << level
+        received = lax.ppermute(parts, axis, [(i, i ^ distance) for i in range(peers)])
+        both = jnp.stack([parts, received])
+        upper = lax.axis_index(axis) >> level & 1
+        parts = jnp.where(upper == 0, both, both[::-1]).reshape(-1, *x.shape)
+    return parts
+
+
+def doubled_up(x, axis, dim):
+    return laid_out(doubled(x, axis), dim)
 
 
 def rank_slots(flat_ids, experts):
@@ -26,10 +48,7 @@
         jnp.bfloat16
     )
     produced = jnp.einsum(
-        "reh,ehd->erd",
-        lax.all_gather(hidden, "token", axis=0, tiled=True),
-        down_w,
-        preferred_element_type=jnp.float32,
+        "reh,ehd->erd", doubled_up(hidden, "token", 0), down_w, preferred_element_type=jnp.float32
     )
     return produced.astype(jnp.bfloat16)
 

time: 167 us -> 172 us (1.030)
  other arithmetic: 7.2 us -> 13.1 us
    ppermute x0 -> x2, waiting for transfers between devices: none -> 20 us  [doubled(): lax.ppermute(parts, axis, [(i, i ^ distance) for i in range(peers)])]
    all_gather x1 -> x0, waiting for transfers between devices: 19.8 us -> none  [expert_block(): lax.all_gather(hidden, 'token', axis=0, tiled=True)]
    another operation x2 -> x6, other arithmetic: 1.19 us -> 6.75 us  [the longest x4 5.56 us: doubled(): both = jnp.stack([parts, received])]
  transfers between devices with their start and end apart: 3 -> 4, of which waited for: 3 -> 4; matrix products, arithmetic and copies ran while one was open for 0% -> 1% of each run, Pallas kernels for 0% -> 0%
where the time goes in v1:
time: 172 us
  waiting for transfers between devices  82.1 us (48%)
  blocking collectives  31.9 us (19%)
  local copies, waits for them, and re-layouts  18.9 us (11%)
  between operations  13.5 us (8%)
  other arithmetic  13.1 us (8%)
  matrix products  7.25 us (4%)
  starting transfers between devices  5.08 us (3%)
    reduce_scatter x1, waiting for transfers between devices, expert_block(): lax.psum_scatter(gate_up_terms(inputs, gate_up_w).astype(jnp.bfloat16), '...  37 us
    all_to_all x1, blocking collectives, per_device(): lax.all_to_all(outgoing, 'expert', split_axis=1, concat_axis=1, tiled=True)  31.9 us
    all_to_all x1, waiting for transfers between devices, per_device(): lax.all_to_all(expert_out.reshape(local_experts, n_expert, capacity, feat...  25 us
    ppermute x2, waiting for transfers between devices, doubled(): lax.ppermute(parts, axis, [(i, i ^ distance) for i in range(peers)])  20 us
    dot_general x1, matrix products, gate_up_terms(): jnp.einsum('erd,edf->ref', inputs, w_gate_up, preferred_element_type=jnp....  6.28 us
    another operation x4, other arithmetic, doubled(): both = jnp.stack([parts, received])  5.56 us
    gather x1, local copies, waits for them, and re-layouts, per_device(): jnp.take(padded, slot_table, axis=0)  5.06 us
    all_to_all x1, starting transfers between devices, per_device(): lax.all_to_all(expert_out.reshape(local_experts, n_expert, capacity, feat...  4.74 us
  transfers between devices with their start and end apart: 4, of which 4 were waited for; matrix products, arithmetic and copies ran while one was open for 1% of the time, Pallas kernels for 0%

profile of v1, /device:TPU:0, one launch (start us, length us, event | category | flops | bytes accessed | tf_op | source)
XLA Modules:
  0.0 171.8 jit_solution(9635469327165170938)
XLA Ops:
  6.5 0.9 copy.33
  7.5 0.1 eq.34
  7.6 0.1 reshape.185
  7.8 1.2 reduce-window.6
  8.9 0.2 slice_reduce_fusion
  9.2 0.1 fusion.9
  9.3 2.4 %scatter_custom_fusion = s32[1024]{0:T(1024)S(1)} fusion(s32[512]{0:T(512)S(1)} %bitcast.48, s32[512]{0:T(512)S(1)} %add_select_fusion.2, s32[]{:T(128)} %constant.86.clone.1), kind=kCustom, calls=%fused_computation.60 | custom fusion | bytes 4100 | tf_op jit(solution)/shard_map/scatter | solution.py:71
  11.9 0.8 concatenate.3
  12.7 5.1 %gather_fusion = bf16[1024,512]{1,0:T(8,128)(2,1)} fusion(bf16[65,512]{1,0:T(8,128)(2,1)S(1)} %concatenate.3, s32[1024]{0:T(1024)S(1)} %fusion.15), kind=kCustom, calls=%fused_computation | custom fusion | bytes 2101248 | tf_op jit(solution)/shard_map/jit(_take)/gather | solution.py:74
  17.8 1.4 copy_select_fusion
  19.2 31.9 %all_to_all.10 = bf16[4,4,64,512]{3,2,0,1:T(8,128)(2,1)S(1)} all-to-all(bf16[4,4,64,512]{3,2,0,1:T(8,128)(2,1)S(1)} %copy_select_fusion), channel_id=1, replica_groups=mesh['groups'=2,'expert'=4,'token'=4] {'expert'}, dimensions={1} | all-to-all | bytes 2097152 | tf_op jit(solution)/shard_map/all_to_all | solution.py:77
  51.2 6.3 %fusion = bf16[256,4,1536]{2,0,1:T(8,128)(2,1)} fusion(bf16[4,256,512]{2,1,0:T(8,128)(2,1)S(1)} %bitcast.44, bf16[4,512,1536]{2,1,0:T(8,128)(2,1)} %param.8), kind=kOutput, calls=%fused_computation.4 | convolution fusion | flops 1612185600 | bytes 10485760 | tf_op jit(solution)/shard_map/erd,edf->ref/dot_general | solution.py:36
  57.5 37.0 %reduce-scatter.2.cloned.1.call-done = bf16[64,4,1536]{2,0,1:T(8,128)(2,1)} async-done(((bf16[256,4,1536]{2,0,1:T(8,128)(2,1)}), bf16[64,4,1536]{2,0,1:T(8,128)(2,1)}) %reduce-scatter.2.cloned.1.call-update) | async-done | bytes 786448 | tf_op jit(solution)/shard_map/reduce_scatter | solution.py:41
  94.5 1.3 convert_element_type.29
  95.8 1.1 copy-done.1
  97.0 1.0 fusion.29
  97.9 1.6 fusion.28
  99.5 0.5 collective-permute-done
  100.0 1.1 pad_maximum_fusion.1
  101.1 1.4 fusion.3
  102.5 0.3 collective-permute-start.1
  102.8 19.6 %collective-permute-done.1 = bf16[2,64,4,768]{3,1,2,0:T(8,128)(2,1)} collective-permute-done((bf16[2,64,4,768]{3,1,2,0:T(8,128)(2,1)}, bf16[2,64,4,768]{3,1,2,0:T(8,128)(2,1)}, u32[]{:S(2)}, u32[]{:S(2)}) %collective-permute-start.1) | collective-permute-done | bytes 786464 | tf_op jit(solution)/shard_map/ppermute | solution.py:18
  122.4 1.5 pad_maximum_fusion
  123.9 0.3 reverse_select_fusion
  124.2 0.1 copy.44
  124.4 1.0 convolution_convert_fusion.1
  125.3 1.1 copy.45
  126.5 4.7 %all-to-all-start.1 = ((bf16[4,4,64,512]{3,2,0,1:T(8,128)(2,1)}), bf16[4,4,64,512]{3,2,0,1:T(8,128)(2,1)}, u32[]{:S(2)}, u32[]{:S(2)}) async-start(bf16[4,4,64,512]{3,2,0,1:T(8,128)(2,1)} %copy.45), calls=%async_computation.2 | async-start | bytes 2097152 | tf_op jit(solution)/shard_map/all_to_all | solution.py:80
  131.5 25.0 %all-to-all-done.1 = bf16[4,4,64,512]{3,2,0,1:T(8,128)(2,1)} async-done(((bf16[4,4,64,512]{3,2,0,1:T(8,128)(2,1)}), bf16[4,4,64,512]{3,2,0,1:T(8,128)(2,1)}, u32[]{:S(2)}, u32[]{:S(2)}) %all-to-all-start.1) | async-done | bytes 1048608 | tf_op jit(solution)/shard_map/all_to_all | solution.py:80
  156.5 2.4 %copy.46 = bf16[4,4,64,512]{3,2,1,0:T(8,128)(2,1)} copy(bf16[4,4,64,512]{3,2,0,1:T(8,128)(2,1)} %all-to-all-done.1) | data formatting | bytes 2097152 | tf_op jit(solution)/shard_map/all_to_all | solution.py:80
  158.8 4.0 %gather_fusion.1 = bf16[512,512]{1,0:T(8,128)(2,1)} fusion(bf16[1024,512]{1,0:T(8,128)(2,1)} %bitcast.42, s32[1024]{0:T(1024)S(1)} %pad_clamp_fusion), kind=kCustom, calls=%fused_computation.1 | custom fusion | bytes 1050624 | tf_op jit(solution)/shard_map/jit(_take)/gather | solution.py:87
  162.9 2.1 %multiply_reduce_fusion = bf16[64,512]{1,0:T(8,128)(2,1)} fusion(bf16[512,512]{1,0:T(8,128)(2,1)} %gather_fusion.1, f32[64,8]{1,0:T(8,128)S(1)} %copy.32, pred[64,8]{1,0:T(8,128)(4,1)S(1)} %compare_and_fusion), kind=kLoop, calls=%fused_computation.10 | loop fusion | flops 1015808 | bytes 592384 | tf_op jit(solution)/shard_map/reduce_sum | solution.py:90
  (23 shorter events, 0.6 us)
Async XLA Ops:
  6.5 117.8 %copy-start = (bf16[4,768,512]{2,1,0:T(8,128)(2,1)S(1)}, bf16[4,768,512]{2,1,0:T(8,128)(2,1)}, u32[]{:S(2)}) copy-start(bf16[4,768,512]{2,1,0:T(8,128)(2,1)} %param.9) | copy-start | bytes 9437188
  6.5 88.0 %reduce-scatter.2.cloned.1.call-start = ((), (), s32[]{:S(2)}) async-start(), calls=%async_computation.3 | async-start | bytes 3932160 | tf_op jit(solution)/shard_map/reduce_scatter | solution.py:41
  95.8 1.2 copy-start.1
  97.9 2.1 %collective-permute-start = (bf16[1,64,4,768]{3,1,2,0:T(8,128)(2,1)}, bf16[1,64,4,768]{3,1,2,0:T(8,128)(2,1)}, u32[]{:S(2)}, u32[]{:S(2)}) collective-permute-start(bf16[1,64,4,768]{3,1,2,0:T(8,128)(2,1)} %fusion.29), channel_id=1, source_target_pairs={{0,1},{1,0},{2,3},{3,2},{4,5},{5,4},{6,7},{7,6},{8,9},{9,8},{10,11... | collective-permute-start | bytes 1179656 | tf_op jit(solution)/shard_map/ppermute | solution.py:18
  102.5 19.9 %collective-permute-start.1 = (bf16[2,64,4,768]{3,1,2,0:T(8,128)(2,1)}, bf16[2,64,4,768]{3,1,2,0:T(8,128)(2,1)}, u32[]{:S(2)}, u32[]{:S(2)}) collective-permute-start(bf16[2,64,4,768]{3,1,2,0:T(8,128)(2,1)} %get-tuple-element.6), channel_id=1, source_target_pairs={{0,2},{1,3},{2,0},{3,1},{4,6},{5,7},{6,4},{7,5},{8,10},{9,11},{10,... | collective-permute-start | bytes 2359304 | tf_op jit(solution)/shard_map/ppermute | solution.py:18
  126.5 4.8 %copy-start.2 = (f32[64,8]{0,1:T(8,128)S(1)}, f32[64,8]{0,1:T(8,128)}, u32[]{:S(2)}) copy-start(f32[64,8]{0,1:T(8,128)} %param.7) | copy-start | bytes 6148
  126.5 30.0 %all-to-all-start.1 = ((bf16[4,4,64,512]{3,2,0,1:T(8,128)(2,1)}), bf16[4,4,64,512]{3,2,0,1:T(8,128)(2,1)}, u32[]{:S(2)}, u32[]{:S(2)}) async-start(bf16[4,4,64,512]{3,2,0,1:T(8,128)(2,1)} %copy.45), calls=%async_computation.2 | async-start | bytes 2097152 | tf_op jit(solution)/shard_map/all_to_all | solution.py:80
Sparse Core Ops, SparseCore 0:
  57.6 36.8 reduce-scatter.1
